TPU v7x, 256 devices: a whole 4x4x8 slice. The times are simulated.
256 devices in a mesh: pipe: 16 (over z, core), expert: 16 (over x, y).
Axes of the slice: x: 4, y: 4, z: 8, core: 2. Of those that a mesh axis runs over, the one named last changes fastest.
Arguments:
- section_inputs: bfloat16 [16, 4, 512, 4096], P('pipe', None, 'expert'), may hold values from -6 to 6
- out_grad: bfloat16 [16, 4, 512, 4096], P('pipe', None, 'expert'), may hold values from -6 to 6
- norm_gain: float32 [8, 4096], replicated, may hold values from 0.5 to 1.5
- route_ids: int32 [16, 4, 512, 1], P('pipe', None, 'expert'), may hold values from 0 to 15; in each aligned block of 32 rows (0 to 31, 32 to 63, ..., all dimensions but the last counted through in order) at most 3 rows name the same one
- route_weight: float32 [16, 4, 512, 1], P('pipe', None, 'expert'), may hold values from 0.2 to 1
- w_gate: bfloat16 [16, 16, 4096, 384], P('pipe', 'expert'), may hold values from -0.09375 to 0.09375
- w_up: bfloat16 [16, 16, 4096, 384], P('pipe', 'expert'), may hold values from -0.09375 to 0.09375
- w_down: bfloat16 [16, 16, 384, 4096], P('pipe', 'expert'), may hold values from -0.21875 to 0.21875
Outputs:
- input_grad: bfloat16 [16, 4, 512, 4096], P('pipe', None, 'expert')
Inputs may be any that keep to these rules, and one draw needn't show every extreme that they name: `route_ids`: each token has exactly one route, naming one expert. In each micro-batch and lane, every aligned block of 32 tokens (the tokens of one device) names one expert at most 3 times, a bound that some block reaches.
All inputs are finite; a program needn't handle non-finite values.
Results may differ from a plain program's by a relative error of at most 0.025.
Values may be sent and summed in bfloat16 or wider, within the bound.
A program may use at most 128 MiB of HBM per device.

v0:
```python
import jax
import jax.numpy as jnp
from jax import lax
from jax.sharding import PartitionSpec as P

EPS = 1e-06


def partner(value, axis, stride):
    mask = 2**stride
    pairs = [(source, source ^ mask) for source in range(lax.axis_size(axis))]
    return lax.ppermute(value, axis, pairs)


def shifted(value, axis, steps):
    count = lax.axis_size(axis)
    leading, last = (max(0, -steps), min(count, count - steps))
    return lax.ppermute(value, axis, [(source, source + steps) for source in range(leading, last)])


def expert_grad(x_rows, d_rows, wg, wu, wd):
    gate = jnp.dot(x_rows, wg, preferred_element_type=jnp.float32)
    up = jnp.dot(x_rows, wu, preferred_element_type=jnp.float32)
    grad_act = jnp.dot(d_rows, wd.T, preferred_element_type=jnp.float32)
    sig = jax.nn.sigmoid(gate)
    dgate = (grad_act * up * sig * (1.0 + gate * (1.0 - sig))).astype(jnp.bfloat16)
    dup = (grad_act * gate * sig).astype(jnp.bfloat16)
    total = jnp.dot(dgate, wg.T, preferred_element_type=jnp.float32) + jnp.dot(
        dup, wu.T, preferred_element_type=jnp.float32
    )
    return total.astype(jnp.bfloat16)


def on_device(section_inputs, out_grad, norm_gain, route_ids, route_weight, w_gate, w_up, w_down):
    lanes = lax.axis_size("pipe")
    sections = lanes // 2
    peers = lax.axis_size("expert")
    lane = lax.axis_index("pipe")
    section = lane // 2
    x = section_inputs[0]
    micro = x.shape[0]
    tok_rows = x.shape[1]
    width = x.shape[2]
    ids = route_ids[0]
    top = ids.shape[2]
    weights = route_weight[0]
    wg = w_gate[0, 0]
    wu = w_up[0, 0]
    wd = w_down[0, 0]
    slots = max(2, min(tok_rows, (3 * tok_rows * top + 2 * peers - 1) // (2 * peers)))
    columns = peers * slots
    norm_weight = lax.dynamic_index_in_dim(norm_gain, section, 0, keepdims=False)
    input_float = x.astype(jnp.float32)
    inverse_norm_scale = lax.rsqrt(
        jnp.mean(input_float * input_float, axis=-1, keepdims=True) + EPS
    )
    unit_input = input_float * inverse_norm_scale
    normed_input = (unit_input * norm_weight).astype(jnp.bfloat16)
    flat_ids = ids.reshape(micro, tok_rows * top)
    onehot = (flat_ids[:, :, None] == jnp.arange(peers, dtype=jnp.int32)).astype(jnp.int32)
    rank = jnp.cumsum(onehot, axis=1) - onehot
    slot_of = jnp.sum(rank * onehot, axis=-1)
    target = flat_ids * slots + slot_of
    picked = (target[:, :, None] == jnp.arange(columns, dtype=jnp.int32)).astype(jnp.float32)
    owner = jnp.arange(tok_rows * top, dtype=jnp.int32) // top
    tokmat = (owner[:, None] == jnp.arange(tok_rows, dtype=jnp.int32)).astype(jnp.float32)
    send_mat = jnp.einsum("mrc,rt->mct", picked, tokmat).astype(jnp.bfloat16)
    flat_weights = weights.reshape(micro, tok_rows * top)
    combine_mat = jnp.einsum("mrc,mr,rt->mtc", picked, flat_weights, tokmat)
    x_send = jnp.einsum(
        "mct,mtd->mcd", send_mat, normed_input, preferred_element_type=jnp.float32
    ).astype(jnp.bfloat16)
    x_send = x_send.reshape(micro, peers, slots, width)

    def step(tau, carry):
        above, section_output = carry
        mb_now = tau - (sections - 1 - section)
        active = jnp.logical_and(mb_now >= 0, mb_now < micro)
        present_rows = jnp.clip(mb_now, 0, micro - 1)
        top_grad = lax.dynamic_index_in_dim(out_grad[0], present_rows, 0, keepdims=False)
        output_gradient = jnp.where(section == sections - 1, top_grad, above)
        send_now = lax.dynamic_index_in_dim(send_mat, present_rows, 0, keepdims=False)
        d_send = jnp.dot(send_now, output_gradient, preferred_element_type=jnp.float32).astype(
            jnp.bfloat16
        )
        d_send = d_send.reshape(peers, slots, width)
        x_now = lax.dynamic_index_in_dim(x_send, present_rows, 0, keepdims=False)
        recv_x, recv_d = (
            lax.all_to_all(x_now, "expert", split_axis=0, concat_axis=0, tiled=True),
            lax.all_to_all(d_send, "expert", split_axis=0, concat_axis=0, tiled=True),
        )
        mine = jnp.stack([recv_x, recv_d])
        other = partner(mine, "pipe", 0)
        rows_x = jnp.stack([recv_x, other[0]])
        rows_d = jnp.stack([recv_d, other[1]])

        def compute():
            out = expert_grad(rows_x.reshape(-1, width), rows_d.reshape(-1, width), wg, wu, wd)
            return out.reshape(2, peers, slots, width)

        def skip():
            return jnp.zeros((2, peers, slots, width), jnp.bfloat16)

        contrib = lax.cond(active, compute, skip)
        from_partner = partner(contrib[1], "pipe", 0)
        summed = (contrib[0].astype(jnp.float32) + from_partner.astype(jnp.float32)).astype(
            jnp.bfloat16
        )
        returned = lax.all_to_all(summed, "expert", split_axis=0, concat_axis=0, tiled=True)
        comb_now = lax.dynamic_index_in_dim(combine_mat, present_rows, 0, keepdims=False)
        dxn = jnp.dot(
            comb_now,
            returned.reshape(columns, width).astype(jnp.float32),
            precision=lax.Precision.HIGHEST,
        )
        weighted_gradient = dxn * norm_weight
        unit_input_present = lax.dynamic_index_in_dim(unit_input, present_rows, 0, keepdims=False)
        scale_now = lax.dynamic_index_in_dim(inverse_norm_scale, present_rows, 0, keepdims=False)
        grad_in = output_gradient.astype(jnp.float32) + scale_now * (
            weighted_gradient
            - unit_input_present
            * jnp.mean(weighted_gradient * unit_input_present, axis=-1, keepdims=True)
        )
        grad_in = grad_in.astype(jnp.bfloat16)
        previous = lax.dynamic_index_in_dim(section_output, present_rows, 0, keepdims=False)
        section_output = lax.dynamic_update_index_in_dim(
            section_output, jnp.where(active, grad_in, previous), present_rows, 0
        )
        incoming = shifted(grad_in, "pipe", -2)
        return (incoming, section_output)

    start_grad = jnp.zeros((tok_rows, width), jnp.bfloat16)
    start_result = jnp.zeros((micro, tok_rows, width), jnp.bfloat16)
    final_grad, final_result = lax.fori_loop(
        0, micro + sections - 1, step, (start_grad, start_result)
    )
    return final_result[None]


def solution(mesh):
    in_specs = (
        P("pipe", None, "expert", None),
        P("pipe", None, "expert", None),
        P(),
        P("pipe", None, "expert", None),
        P("pipe", None, "expert", None),
        P("pipe", "expert", None, None),
        P("pipe", "expert", None, None),
        P("pipe", "expert", None, None),
    )
    out_specs = P("pipe", None, "expert", None)
    return jax.shard_map(
        on_device, mesh=mesh, in_specs=in_specs, out_specs=out_specs, check_vma=False
    )
```

profile of v0, /device:TPU:8, one launch (start us, length us, event | category | flops | bytes accessed | tf_op | source)
XLA Modules:
  0.0 1169.4 jit_solution(1968684166901219924)
XLA Ops:
  14.9 1154.4 %while.17 = (s32[]{:T(128)}, bf16[32,4096]{1,0:T(8,128)(2,1)S(1)}, bf16[4,32,4096]{2,1,0:T(8,128)(2,1)}, pred[]{:T(512)}, s32[]{:T(128)}, /*index=5*/bf16[1,4,32...) while((s32[]{:T(128)}, bf16[32,4096]{1,0:T(8,128)(2,1)S(1)}, ...), condition=%wide.region_7.8_spmd, body=%wide.region_3.7_spmd.sunk | while | flops 1603141632 | bytes 61354832 | solution.py:134
  36.9 13.8 %all_to_all.36 = bf16[16,3,4096]{2,1,0:T(4,128)(2,1)S(1)} all-to-all(bf16[16,3,4096]{2,1,0:T(4,128)(2,1)} %dynamic-slice_bitcast_fusion.2), channel_id=1, replica_groups=mesh['pipe'=16,'expert'=16] {'expert'}, dimensions={0} | all-to-all | bytes 786432 | tf_op jit(solution)/shard_map/while/body/eval_jaxpr/all_to_all | solution.py:89
  77.4 9.2 all-to-all-done.2
  120.4 13.6 %all_to_all.36 = bf16[16,3,4096]{2,1,0:T(4,128)(2,1)S(1)} all-to-all(bf16[16,3,4096]{2,1,0:T(4,128)(2,1)} %dynamic-slice_bitcast_fusion.2), channel_id=1, replica_groups=mesh['pipe'=16,'expert'=16] {'expert'}, dimensions={0} | all-to-all | bytes 786432 | tf_op jit(solution)/shard_map/while/body/eval_jaxpr/all_to_all | solution.py:89
  160.6 9.2 all-to-all-done.2
  203.7 13.6 %all_to_all.36 = bf16[16,3,4096]{2,1,0:T(4,128)(2,1)S(1)} all-to-all(bf16[16,3,4096]{2,1,0:T(4,128)(2,1)} %dynamic-slice_bitcast_fusion.2), channel_id=1, replica_groups=mesh['pipe'=16,'expert'=16] {'expert'}, dimensions={0} | all-to-all | bytes 786432 | tf_op jit(solution)/shard_map/while/body/eval_jaxpr/all_to_all | solution.py:89
  243.9 9.2 all-to-all-done.2
  287.0 13.6 %all_to_all.36 = bf16[16,3,4096]{2,1,0:T(4,128)(2,1)S(1)} all-to-all(bf16[16,3,4096]{2,1,0:T(4,128)(2,1)} %dynamic-slice_bitcast_fusion.2), channel_id=1, replica_groups=mesh['pipe'=16,'expert'=16] {'expert'}, dimensions={0} | all-to-all | bytes 786432 | tf_op jit(solution)/shard_map/while/body/eval_jaxpr/all_to_all | solution.py:89
  327.3 9.2 all-to-all-done.2
  371.8 13.6 %all_to_all.36 = bf16[16,3,4096]{2,1,0:T(4,128)(2,1)S(1)} all-to-all(bf16[16,3,4096]{2,1,0:T(4,128)(2,1)} %dynamic-slice_bitcast_fusion.2), channel_id=1, replica_groups=mesh['pipe'=16,'expert'=16] {'expert'}, dimensions={0} | all-to-all | bytes 786432 | tf_op jit(solution)/shard_map/while/body/eval_jaxpr/all_to_all | solution.py:89
  455.9 13.6 %all_to_all.36 = bf16[16,3,4096]{2,1,0:T(4,128)(2,1)S(1)} all-to-all(bf16[16,3,4096]{2,1,0:T(4,128)(2,1)} %dynamic-slice_bitcast_fusion.2), channel_id=1, replica_groups=mesh['pipe'=16,'expert'=16] {'expert'}, dimensions={0} | all-to-all | bytes 786432 | tf_op jit(solution)/shard_map/while/body/eval_jaxpr/all_to_all | solution.py:89
  540.0 13.6 %all_to_all.36 = bf16[16,3,4096]{2,1,0:T(4,128)(2,1)S(1)} all-to-all(bf16[16,3,4096]{2,1,0:T(4,128)(2,1)} %dynamic-slice_bitcast_fusion.2), channel_id=1, replica_groups=mesh['pipe'=16,'expert'=16] {'expert'}, dimensions={0} | all-to-all | bytes 786432 | tf_op jit(solution)/shard_map/while/body/eval_jaxpr/all_to_all | solution.py:89
  596.7 152.0 %collective-permute-done.2 = bf16[32,4096]{1,0:T(8,128)(2,1)S(1)} collective-permute-done((bf16[32,4096]{1,0:T(8,128)(2,1)}, bf16[32,4096]{1,0:T(8,128)(2,1)S(1)}, u32[]{:S(2)}, u32[]{:S(2)}) %collective-permute-start.2) | collective-permute-done | bytes 262176 | tf_op jit(solution)/shard_map/while/body/eval_jaxpr/ppermute | solution.py:18
  767.7 13.6 %all_to_all.36 = bf16[16,3,4096]{2,1,0:T(4,128)(2,1)S(1)} all-to-all(bf16[16,3,4096]{2,1,0:T(4,128)(2,1)} %dynamic-slice_bitcast_fusion.2), channel_id=1, replica_groups=mesh['pipe'=16,'expert'=16] {'expert'}, dimensions={0} | all-to-all | bytes 786432 | tf_op jit(solution)/shard_map/while/body/eval_jaxpr/all_to_all | solution.py:89
  793.8 22.7 %conditional.2 = (bf16[2,16,3,4096]{3,2,1,0:T(4,128)(2,1)}) conditional(s32[]{:T(128)} %convert_element_type.133, () %tuple.58, (bf16[2,16,3,4096]{3,2,1,0:T(4,128)(2,1)}, bf16[384,4096]{1,0:T(8,128)(2,1)}, bf16[2,16,3,4096]{3,2,1,0:T(4,128)(2,1)}, bf16[4096,384]{1,0:T(8,128)(2,1)S(1)}, bf16[4096,384]{1,0:T(8,128)(2,1)}) %tuple.59), branch_computations={%region_4.4_spmd, %region_5.5_spmd} | conditional | flops 1511325696 | bytes 27623432 | solution.py:104
  829.2 9.2 all-to-all-done.2
  873.0 13.6 %all_to_all.36 = bf16[16,3,4096]{2,1,0:T(4,128)(2,1)S(1)} all-to-all(bf16[16,3,4096]{2,1,0:T(4,128)(2,1)} %dynamic-slice_bitcast_fusion.2), channel_id=1, replica_groups=mesh['pipe'=16,'expert'=16] {'expert'}, dimensions={0} | all-to-all | bytes 786432 | tf_op jit(solution)/shard_map/while/body/eval_jaxpr/all_to_all | solution.py:89
  899.2 22.7 %conditional.2 = (bf16[2,16,3,4096]{3,2,1,0:T(4,128)(2,1)}) conditional(s32[]{:T(128)} %convert_element_type.133, () %tuple.58, (bf16[2,16,3,4096]{3,2,1,0:T(4,128)(2,1)}, bf16[384,4096]{1,0:T(8,128)(2,1)}, bf16[2,16,3,4096]{3,2,1,0:T(4,128)(2,1)}, bf16[4096,384]{1,0:T(8,128)(2,1)S(1)}, bf16[4096,384]{1,0:T(8,128)(2,1)}) %tuple.59), branch_computations={%region_4.4_spmd, %region_5.5_spmd} | conditional | flops 1511325696 | bytes 27623432 | solution.py:104
  934.5 9.2 all-to-all-done.2
  978.4 13.6 %all_to_all.36 = bf16[16,3,4096]{2,1,0:T(4,128)(2,1)S(1)} all-to-all(bf16[16,3,4096]{2,1,0:T(4,128)(2,1)} %dynamic-slice_bitcast_fusion.2), channel_id=1, replica_groups=mesh['pipe'=16,'expert'=16] {'expert'}, dimensions={0} | all-to-all | bytes 786432 | tf_op jit(solution)/shard_map/while/body/eval_jaxpr/all_to_all | solution.py:89
  1004.5 22.7 %conditional.2 = (bf16[2,16,3,4096]{3,2,1,0:T(4,128)(2,1)}) conditional(s32[]{:T(128)} %convert_element_type.133, () %tuple.58, (bf16[2,16,3,4096]{3,2,1,0:T(4,128)(2,1)}, bf16[384,4096]{1,0:T(8,128)(2,1)}, bf16[2,16,3,4096]{3,2,1,0:T(4,128)(2,1)}, bf16[4096,384]{1,0:T(8,128)(2,1)S(1)}, bf16[4096,384]{1,0:T(8,128)(2,1)}) %tuple.59), branch_computations={%region_4.4_spmd, %region_5.5_spmd} | conditional | flops 1511325696 | bytes 27623432 | solution.py:104
  1083.8 13.6 %all_to_all.36 = bf16[16,3,4096]{2,1,0:T(4,128)(2,1)S(1)} all-to-all(bf16[16,3,4096]{2,1,0:T(4,128)(2,1)} %dynamic-slice_bitcast_fusion.2), channel_id=1, replica_groups=mesh['pipe'=16,'expert'=16] {'expert'}, dimensions={0} | all-to-all | bytes 786432 | tf_op jit(solution)/shard_map/while/body/eval_jaxpr/all_to_all | solution.py:89
  1109.9 22.7 %conditional.2 = (bf16[2,16,3,4096]{3,2,1,0:T(4,128)(2,1)}) conditional(s32[]{:T(128)} %convert_element_type.133, () %tuple.58, (bf16[2,16,3,4096]{3,2,1,0:T(4,128)(2,1)}, bf16[384,4096]{1,0:T(8,128)(2,1)}, bf16[2,16,3,4096]{3,2,1,0:T(4,128)(2,1)}, bf16[4096,384]{1,0:T(8,128)(2,1)S(1)}, bf16[4096,384]{1,0:T(8,128)(2,1)}) %tuple.59), branch_computations={%region_4.4_spmd, %region_5.5_spmd} | conditional | flops 1511325696 | bytes 27623432 | solution.py:104
  1145.3 9.2 all-to-all-done.2
  (447 shorter events, 811.5 us)
Async XLA Ops:
  19.3 17.6 %all-to-all-start.1 = ((bf16[16,3,4096]{2,1,0:T(4,128)(2,1)}), bf16[16,3,4096]{2,1,0:T(4,128)(2,1)}, u32[]{:S(2)}, u32[]{:S(2)}) async-start(bf16[16,3,4096]{2,1,0:T(4,128)(2,1)} %reshape.84), calls=%async_computation.1 | async-start | bytes 1048576 | tf_op jit(solution)/shard_map/while/body/eval_jaxpr/all_to_all | solution.py:90
  70.1 16.5 %all-to-all-start.2 = ((bf16[16,3,4096]{2,1,0:T(4,128)(2,1)}), bf16[16,3,4096]{2,1,0:T(4,128)(2,1)}, u32[]{:S(2)}, u32[]{:S(2)}) async-start(bf16[16,3,4096]{2,1,0:T(4,128)(2,1)} %fusion.60), calls=%async_computation.2 | async-start | bytes 1048576 | tf_op jit(solution)/shard_map/while/body/eval_jaxpr/all_to_all | solution.py:109
  105.8 14.6 %all-to-all-start.1 = ((bf16[16,3,4096]{2,1,0:T(4,128)(2,1)}), bf16[16,3,4096]{2,1,0:T(4,128)(2,1)}, u32[]{:S(2)}, u32[]{:S(2)}) async-start(bf16[16,3,4096]{2,1,0:T(4,128)(2,1)} %reshape.84), calls=%async_computation.1 | async-start | bytes 1048576 | tf_op jit(solution)/shard_map/while/body/eval_jaxpr/all_to_all | solution.py:90
  153.4 16.5 %all-to-all-start.2 = ((bf16[16,3,4096]{2,1,0:T(4,128)(2,1)}), bf16[16,3,4096]{2,1,0:T(4,128)(2,1)}, u32[]{:S(2)}, u32[]{:S(2)}) async-start(bf16[16,3,4096]{2,1,0:T(4,128)(2,1)} %fusion.60), calls=%async_computation.2 | async-start | bytes 1048576 | tf_op jit(solution)/shard_map/while/body/eval_jaxpr/all_to_all | solution.py:109
  189.1 14.6 %all-to-all-start.1 = ((bf16[16,3,4096]{2,1,0:T(4,128)(2,1)}), bf16[16,3,4096]{2,1,0:T(4,128)(2,1)}, u32[]{:S(2)}, u32[]{:S(2)}) async-start(bf16[16,3,4096]{2,1,0:T(4,128)(2,1)} %reshape.84), calls=%async_computation.1 | async-start | bytes 1048576 | tf_op jit(solution)/shard_map/while/body/eval_jaxpr/all_to_all | solution.py:90
  236.7 16.5 %all-to-all-start.2 = ((bf16[16,3,4096]{2,1,0:T(4,128)(2,1)}), bf16[16,3,4096]{2,1,0:T(4,128)(2,1)}, u32[]{:S(2)}, u32[]{:S(2)}) async-start(bf16[16,3,4096]{2,1,0:T(4,128)(2,1)} %fusion.60), calls=%async_computation.2 | async-start | bytes 1048576 | tf_op jit(solution)/shard_map/while/body/eval_jaxpr/all_to_all | solution.py:109
  272.4 14.7 %all-to-all-start.1 = ((bf16[16,3,4096]{2,1,0:T(4,128)(2,1)}), bf16[16,3,4096]{2,1,0:T(4,128)(2,1)}, u32[]{:S(2)}, u32[]{:S(2)}) async-start(bf16[16,3,4096]{2,1,0:T(4,128)(2,1)} %reshape.84), calls=%async_computation.1 | async-start | bytes 1048576 | tf_op jit(solution)/shard_map/while/body/eval_jaxpr/all_to_all | solution.py:90
  320.0 16.5 %all-to-all-start.2 = ((bf16[16,3,4096]{2,1,0:T(4,128)(2,1)}), bf16[16,3,4096]{2,1,0:T(4,128)(2,1)}, u32[]{:S(2)}, u32[]{:S(2)}) async-start(bf16[16,3,4096]{2,1,0:T(4,128)(2,1)} %fusion.60), calls=%async_computation.2 | async-start | bytes 1048576 | tf_op jit(solution)/shard_map/while/body/eval_jaxpr/all_to_all | solution.py:109
  342.5 10.4 collective-permute-start.2
  357.1 14.7 %all-to-all-start.1 = ((bf16[16,3,4096]{2,1,0:T(4,128)(2,1)}), bf16[16,3,4096]{2,1,0:T(4,128)(2,1)}, u32[]{:S(2)}, u32[]{:S(2)}) async-start(bf16[16,3,4096]{2,1,0:T(4,128)(2,1)} %reshape.84), calls=%async_computation.1 | async-start | bytes 1048576 | tf_op jit(solution)/shard_map/while/body/eval_jaxpr/all_to_all | solution.py:90
  404.8 16.5 %all-to-all-start.2 = ((bf16[16,3,4096]{2,1,0:T(4,128)(2,1)}), bf16[16,3,4096]{2,1,0:T(4,128)(2,1)}, u32[]{:S(2)}, u32[]{:S(2)}) async-start(bf16[16,3,4096]{2,1,0:T(4,128)(2,1)} %fusion.60), calls=%async_computation.2 | async-start | bytes 1048576 | tf_op jit(solution)/shard_map/while/body/eval_jaxpr/all_to_all | solution.py:109
  441.2 14.7 %all-to-all-start.1 = ((bf16[16,3,4096]{2,1,0:T(4,128)(2,1)}), bf16[16,3,4096]{2,1,0:T(4,128)(2,1)}, u32[]{:S(2)}, u32[]{:S(2)}) async-start(bf16[16,3,4096]{2,1,0:T(4,128)(2,1)} %reshape.84), calls=%async_computation.1 | async-start | bytes 1048576 | tf_op jit(solution)/shard_map/while/body/eval_jaxpr/all_to_all | solution.py:90
  488.9 16.5 %all-to-all-start.2 = ((bf16[16,3,4096]{2,1,0:T(4,128)(2,1)}), bf16[16,3,4096]{2,1,0:T(4,128)(2,1)}, u32[]{:S(2)}, u32[]{:S(2)}) async-start(bf16[16,3,4096]{2,1,0:T(4,128)(2,1)} %fusion.60), calls=%async_computation.2 | async-start | bytes 1048576 | tf_op jit(solution)/shard_map/while/body/eval_jaxpr/all_to_all | solution.py:109
  525.3 14.7 %all-to-all-start.1 = ((bf16[16,3,4096]{2,1,0:T(4,128)(2,1)}), bf16[16,3,4096]{2,1,0:T(4,128)(2,1)}, u32[]{:S(2)}, u32[]{:S(2)}) async-start(bf16[16,3,4096]{2,1,0:T(4,128)(2,1)} %reshape.84), calls=%async_computation.1 | async-start | bytes 1048576 | tf_op jit(solution)/shard_map/while/body/eval_jaxpr/all_to_all | solution.py:90
  573.0 16.5 %all-to-all-start.2 = ((bf16[16,3,4096]{2,1,0:T(4,128)(2,1)}), bf16[16,3,4096]{2,1,0:T(4,128)(2,1)}, u32[]{:S(2)}, u32[]{:S(2)}) async-start(bf16[16,3,4096]{2,1,0:T(4,128)(2,1)} %fusion.60), calls=%async_computation.2 | async-start | bytes 1048576 | tf_op jit(solution)/shard_map/while/body/eval_jaxpr/all_to_all | solution.py:109
  595.5 153.3 %collective-permute-start.2 = (bf16[32,4096]{1,0:T(8,128)(2,1)}, bf16[32,4096]{1,0:T(8,128)(2,1)S(1)}, u32[]{:S(2)}, u32[]{:S(2)}) collective-permute-start(bf16[32,4096]{1,0:T(8,128)(2,1)} %get-tuple-element.540), channel_id=1, source_target_pairs={{32,0},{48,16},{64,32},{80,48},{96,64},{112,80},{128,96},{144,112}... | collective-permute-start | bytes 786440 | tf_op jit(solution)/shard_map/while/body/eval_jaxpr/ppermute | solution.py:18
  752.9 14.7 %all-to-all-start.1 = ((bf16[16,3,4096]{2,1,0:T(4,128)(2,1)}), bf16[16,3,4096]{2,1,0:T(4,128)(2,1)}, u32[]{:S(2)}, u32[]{:S(2)}) async-start(bf16[16,3,4096]{2,1,0:T(4,128)(2,1)} %reshape.84), calls=%async_computation.1 | async-start | bytes 1048576 | tf_op jit(solution)/shard_map/while/body/eval_jaxpr/all_to_all | solution.py:90
  821.9 16.5 %all-to-all-start.2 = ((bf16[16,3,4096]{2,1,0:T(4,128)(2,1)}), bf16[16,3,4096]{2,1,0:T(4,128)(2,1)}, u32[]{:S(2)}, u32[]{:S(2)}) async-start(bf16[16,3,4096]{2,1,0:T(4,128)(2,1)} %fusion.60), calls=%async_computation.2 | async-start | bytes 1048576 | tf_op jit(solution)/shard_map/while/body/eval_jaxpr/all_to_all | solution.py:109
  858.3 14.7 %all-to-all-start.1 = ((bf16[16,3,4096]{2,1,0:T(4,128)(2,1)}), bf16[16,3,4096]{2,1,0:T(4,128)(2,1)}, u32[]{:S(2)}, u32[]{:S(2)}) async-start(bf16[16,3,4096]{2,1,0:T(4,128)(2,1)} %reshape.84), calls=%async_computation.1 | async-start | bytes 1048576 | tf_op jit(solution)/shard_map/while/body/eval_jaxpr/all_to_all | solution.py:90
  927.3 16.5 %all-to-all-start.2 = ((bf16[16,3,4096]{2,1,0:T(4,128)(2,1)}), bf16[16,3,4096]{2,1,0:T(4,128)(2,1)}, u32[]{:S(2)}, u32[]{:S(2)}) async-start(bf16[16,3,4096]{2,1,0:T(4,128)(2,1)} %fusion.60), calls=%async_computation.2 | async-start | bytes 1048576 | tf_op jit(solution)/shard_map/while/body/eval_jaxpr/all_to_all | solution.py:109
  963.7 14.7 %all-to-all-start.1 = ((bf16[16,3,4096]{2,1,0:T(4,128)(2,1)}), bf16[16,3,4096]{2,1,0:T(4,128)(2,1)}, u32[]{:S(2)}, u32[]{:S(2)}) async-start(bf16[16,3,4096]{2,1,0:T(4,128)(2,1)} %reshape.84), calls=%async_computation.1 | async-start | bytes 1048576 | tf_op jit(solution)/shard_map/while/body/eval_jaxpr/all_to_all | solution.py:90
  1032.7 16.5 %all-to-all-start.2 = ((bf16[16,3,4096]{2,1,0:T(4,128)(2,1)}), bf16[16,3,4096]{2,1,0:T(4,128)(2,1)}, u32[]{:S(2)}, u32[]{:S(2)}) async-start(bf16[16,3,4096]{2,1,0:T(4,128)(2,1)} %fusion.60), calls=%async_computation.2 | async-start | bytes 1048576 | tf_op jit(solution)/shard_map/while/body/eval_jaxpr/all_to_all | solution.py:109
  1069.0 14.7 %all-to-all-start.1 = ((bf16[16,3,4096]{2,1,0:T(4,128)(2,1)}), bf16[16,3,4096]{2,1,0:T(4,128)(2,1)}, u32[]{:S(2)}, u32[]{:S(2)}) async-start(bf16[16,3,4096]{2,1,0:T(4,128)(2,1)} %reshape.84), calls=%async_computation.1 | async-start | bytes 1048576 | tf_op jit(solution)/shard_map/while/body/eval_jaxpr/all_to_all | solution.py:90
  1138.0 16.5 %all-to-all-start.2 = ((bf16[16,3,4096]{2,1,0:T(4,128)(2,1)}), bf16[16,3,4096]{2,1,0:T(4,128)(2,1)}, u32[]{:S(2)}, u32[]{:S(2)}) async-start(bf16[16,3,4096]{2,1,0:T(4,128)(2,1)} %fusion.60), calls=%async_computation.2 | async-start | bytes 1048576 | tf_op jit(solution)/shard_map/while/body/eval_jaxpr/all_to_all | solution.py:109
  (81 other events, 797.6 us)
where the time goes:
time: 1180 us; the launch traced here: 1170 us
  waiting for transfers between devices  450 us (38%)
  local copies, waits for them, and re-layouts  204 us (17%)
  blocking collectives  150 us (13%)
  starting transfers between devices  141 us (12%)
  other arithmetic  118 us (10%)
  matrix products  105 us (9%)
    ppermute x11, waiting for transfers between devices, shifted(): lax.ppermute(value, axis, [(source, source + steps) for source in range(l...  234 us
    all_to_all x11, blocking collectives, step(): lax.all_to_all(x_now, 'expert', split_axis=0, concat_axis=0, tiled=True)  150 us
    all_to_all x11, waiting for transfers between devices, step(): lax.all_to_all(summed, 'expert', split_axis=0, concat_axis=0, tiled=True)  102 us
    all_to_all x11, waiting for transfers between devices, step(): lax.all_to_all(d_send, 'expert', split_axis=0, concat_axis=0, tiled=True)  79.2 us
    all_to_all x11, starting transfers between devices, step(): lax.all_to_all(d_send, 'expert', split_axis=0, concat_axis=0, tiled=True)  63.1 us
    all_to_all x11, starting transfers between devices, step(): lax.all_to_all(summed, 'expert', split_axis=0, concat_axis=0, tiled=True)  61.2 us
    another operation x11, other arithmetic, step(): rows_x = jnp.stack([recv_x, other[0]])  43.1 us
    ppermute x22, waiting for transfers between devices, partner(): return lax.ppermute(value, axis, pairs)  35.1 us
  transfers between devices with their start and end apart: 55, of which 55 were waited for; matrix products, arithmetic and copies ran while one was open for 5% of the time, Pallas kernels for 0%

commit v1 on v0

v1 whole, which is shorter than its diff:
```python
import jax
import jax.numpy as jnp
from jax import lax
from jax.experimental import pallas as pl
from jax.experimental.pallas import tpu as pltpu
from jax.sharding import PartitionSpec as P

EPS = 1e-06
MESH = pl.DeviceIdType.MESH
BF = jnp.bfloat16
F32 = jnp.float32
CAP = 3
NC = 2


def dot_t(a, b):
    return lax.dot_general(a, b, (((1,), (1,)), ((), ())), preferred_element_type=F32)


def make_kernel(MB, T, D, FH, LANES, PEERS):
    SEC = LANES // 2
    SLOTS = PEERS * CAP
    SUB = D // 128
    CS = SUB // NC
    CD = D // NC
    FF = 2 * FH

    def kernel(tok_ref, cidx_ref, slotup_ref, x_hbm, og_hbm, wtab_hbm, gain_ref, wg_hbm, wu_hbm, wd_hbm, out_hbm,
               xv, ov, xrow, orow, sendx, recvx, sendd, recvd, sendr, xstd, xn, dys, ostd, fa, fb, fc, rs, wtab, wrecv, wrow,
               wg, wu, wd, fin, outstd,
               ret00, ret01, ret10, ret11, ret20, ret21, ret30, ret31,
               in_sem, wl_sem, wrs_sem, wrr_sem, ts_sem, tr_sem, xs_sem, xr_sem, ds_sem, dr_sem, rsnd_sem, rr_sem,
               os_sem, or_sem):
        rets = ((ret00, ret01), (ret10, ret11), (ret20, ret21), (ret30, ret31))
        p = lax.axis_index("pipe")
        e = lax.axis_index("expert")
        s = p // 2
        h = p % 2
        down = (p + LANES - 2) % LANES
        up = (p + 2) % LANES
        mate = p + 1 - 2 * h
        top = s == SEC - 1

        def local_in(src, dst, i):
            return pltpu.make_async_copy(src, dst, in_sem.at[i])

        in_x = local_in(x_hbm, xv, 0)
        in_o = local_in(og_hbm, ov, 1)
        in_t = local_in(wtab_hbm, wtab, 2)
        in_x.start()
        in_t.start()
        in_o.start()
        gcol = pl.ds(pl.multiple_of(h * FH, 128), FH)
        drow = pl.ds(pl.multiple_of(h * FH, 128), FH)
        lw = (
            pltpu.make_async_copy(wg_hbm, wg.at[:, gcol], wl_sem.at[0]),
            pltpu.make_async_copy(wu_hbm, wu.at[:, gcol], wl_sem.at[1]),
            pltpu.make_async_copy(wd_hbm, wd.at[drow, :], wl_sem.at[2]),
        )
        for c in lw:
            c.start()

        barrier = pltpu.get_barrier_semaphore()

        def sig_plane(k, _):
            pl.semaphore_signal(barrier, inc=1, device_id=(p, (e + k) % PEERS), device_id_type=MESH)
            return 0

        lax.fori_loop(1, PEERS, sig_plane, 0)

        def sig_z(k, _):
            peer = (e + k) % PEERS
            pl.semaphore_signal(barrier, inc=1, device_id=(down, peer), device_id_type=MESH)
            pl.semaphore_signal(barrier, inc=1, device_id=(up, peer), device_id_type=MESH)
            return 0

        lax.fori_loop(0, PEERS, sig_z, 0)
        pl.semaphore_signal(barrier, inc=1, device_id=(mate, e), device_id_type=MESH)
        pl.semaphore_wait(barrier, PEERS - 1 + 2 * PEERS + 1)

        def rcopy(src, dst, ssem, rsem, dev):
            return pltpu.make_async_remote_copy(
                src_ref=src, dst_ref=dst, send_sem=ssem, recv_sem=rsem, device_id=dev, device_id_type=MESH
            )

        rw = (
            rcopy(wg_hbm, wg.at[:, gcol], wrs_sem.at[0], wrr_sem.at[0], (mate, e)),
            rcopy(wu_hbm, wu.at[:, gcol], wrs_sem.at[1], wrr_sem.at[1], (mate, e)),
            rcopy(wd_hbm, wd.at[drow, :], wrs_sem.at[2], wrr_sem.at[2], (mate, e)),
        )
        for c in rw:
            c.start()

        mine = pl.ds(e * CAP, CAP)

        def send_x(m):
            for k in range(SLOTS):
                sendx[m, k] = xrow[m * T + tok_ref[m * SLOTS + k]]
            recvx[m, mine] = sendx[m, mine]

            def go(k, _):
                peer = (e + k) % PEERS
                rcopy(sendx.at[m, pl.ds(peer * CAP, CAP)], recvx.at[m, mine], xs_sem.at[m], xr_sem.at[m], (p, peer)).start()
                return 0

            lax.fori_loop(1, PEERS, go, 0)

        def wait_x(m):
            return rcopy(
                sendx.at[m, pl.ds(0, SLOTS - CAP)], recvx.at[m, pl.ds(0, SLOTS - CAP)], xs_sem.at[m], xr_sem.at[m], (p, e)
            )

        def send_d(m, c):
            recvd[m, c, mine] = sendd[m, c, mine]

            def go(k, _):
                peer = (e + k) % PEERS
                rcopy(
                    sendd.at[m, c, pl.ds(peer * CAP, CAP)], recvd.at[m, c, mine], ds_sem.at[m, c], dr_sem.at[m, c], (p, peer)
                ).start()
                return 0

            lax.fori_loop(1, PEERS, go, 0)

        def wait_d(m, c):
            return rcopy(
                sendd.at[m, c, pl.ds(0, SLOTS - CAP)],
                recvd.at[m, c, pl.ds(0, SLOTS - CAP)],
                ds_sem.at[m, c],
                dr_sem.at[m, c],
                (p, e),
            )

        def send_r(m, c):
            def go(k, _):
                peer = (e + k) % PEERS
                rcopy(
                    sendr.at[m, c, pl.ds(peer * CAP, CAP)],
                    rets[m][c].at[mine],
                    rsnd_sem.at[m, c],
                    rr_sem.at[m, c],
                    (down, peer),
                ).start()
                return 0

            lax.fori_loop(0, PEERS, go, 0)

        def wait_r(m, c):
            return rcopy(sendr.at[m, c], rets[m][c], rsnd_sem.at[m, c], rr_sem.at[m, c], (down, e))

        def send_out(m):
            return rcopy(outstd.at[m], out_hbm.at[m], os_sem.at[m], or_sem.at[m], (up, e))

        in_x.wait()
        in_o.wait()
        in_t.wait()

        def tables(k, _):
            peer = (e + k) % PEERS
            rcopy(wtab.at[peer], wrecv.at[e], ts_sem, tr_sem, (p, peer)).start()
            return 0

        lax.fori_loop(1, PEERS, tables, 0)
        wrecv[e] = wtab[e]
        tabs = rcopy(wtab.at[pl.ds(0, PEERS - 1)], wrecv.at[pl.ds(0, PEERS - 1)], ts_sem, tr_sem, (p, e))

        for m in range(MB):
            xrow[pl.ds(m * T, T)] = xv[m].reshape(T, SUB, 128)
            send_x(m)

            @pl.when(top)
            def _():
                orow[pl.ds(m * T, T)] = ov[m].reshape(T, SUB, 128)
                for c in range(NC):
                    for k in range(SLOTS):
                        sendd[m, c, k] = orow[m * T + tok_ref[m * SLOTS + k], pl.ds(c * CS, CS), :]
                    send_d(m, c)

        gain = gain_ref.at[pl.ds(s, 1), :]
        QD = 512

        for c in lw:
            c.wait()
        for c in rw:
            c.wait_recv()
        tabs.wait_recv()

        def factors(m, _):
            wait_x(m).wait_recv()
            xstd[m] = recvx[m].reshape(SLOTS, D)
            for j in range(CAP):
                wrow[pl.ds(j, PEERS, stride=CAP), :] = wrecv[:, m * CAP + j, :]
            w = wrow[:, :1]

            def sq(i, acc):
                col = pl.ds(pl.multiple_of(i * QD, QD), QD)
                v = xstd[m, :, col].astype(F32)
                return acc + jnp.sum(v * v, axis=-1, keepdims=True)

            total = lax.fori_loop(0, D // QD, sq, jnp.zeros((SLOTS, 1), F32))
            r = lax.rsqrt(total * (1.0 / D) + EPS)
            rs[m] = jnp.broadcast_to(r, (SLOTS, 128))

            def norm(i, _):
                col = pl.ds(pl.multiple_of(i * QD, QD), QD)
                xn[:, col] = (xstd[m, :, col].astype(F32) * r * gain[:, col]).astype(BF)
                return 0

            lax.fori_loop(0, D // QD, norm, 0)
            gate = jnp.dot(xn[...], wg[...], preferred_element_type=F32)
            upv = jnp.dot(xn[...], wu[...], preferred_element_type=F32)
            q = jax.nn.sigmoid(gate)
            a = upv * q * (1.0 + gate * (1.0 - q))
            b = gate * q
            fa[m] = w * a
            fb[m] = w * b
            fc[m] = w * (a * gate + b * upv) * (1.0 / D)
            return 0

        lax.fori_loop(0, jnp.where(top, 1, MB), factors, 0)

        def home(m):
            for c in range(NC):
                wait_r(m, c).wait_recv()
                for k in range(SLOTS):
                    sendd[m, c, k] = rets[m][c][cidx_ref[m * SLOTS + k]]
                send_d(m, c)

        def output(m):
            for c in range(NC):
                for t in range(T):
                    fin[t, pl.ds(c * CS, CS), :] = rets[m][c][slotup_ref[m * T + t]]
            outstd[m] = fin[...].reshape(T, D)
            send_out(m).start()

        def chain(m, _):
            for i in range(MB):

                @pl.when(jnp.logical_and(m == i, jnp.logical_not(top)))
                def _():
                    home(i)

            lax.fori_loop(m + 1, jnp.where(jnp.logical_and(top, m < MB - 1), m + 2, m + 1), factors, 0)
            da = jnp.zeros((SLOTS, FF), F32)
            for c in range(NC):
                wait_d(m, c).wait_recv()
                dys[:, c * CD:(c + 1) * CD] = recvd[m, c].reshape(SLOTS, CD)
                da = da + dot_t(dys[:, c * CD:(c + 1) * CD], wd[:, c * CD:(c + 1) * CD])
            dg = (da * fa[m]).astype(BF)
            du = (da * fb[m]).astype(BF)
            r = rs[m][:, :1]
            mean = jnp.sum(da * fc[m], axis=-1, keepdims=True) * (r * r)
            for c in range(NC):
                for i in range(CD // QD):
                    col = pl.ds(c * CD + i * QD, QD)
                    con = dot_t(dg, wg[col, :]) + dot_t(du, wu[col, :])
                    res = dys[:, col].astype(F32) + (con * gain[:, col]) * r - xstd[m, :, col].astype(F32) * mean
                    ostd[:, pl.ds(i * QD, QD)] = res.astype(BF)
                sendr[m, c] = ostd[...].reshape(SLOTS, CS, 128)
                for i in range(MB):

                    @pl.when(m == i)
                    def _():
                        send_r(i, c)

            for i in range(MB):

                @pl.when(jnp.logical_and(m == i, jnp.logical_not(top)))
                def _():
                    output(i)

            return 0

        lax.fori_loop(0, MB, chain, 0)

        @pl.when(top)
        def _():
            for m in range(MB):
                for c in range(NC):
                    wait_r(m, c).wait_recv()
                output(m)

        for c in rw:
            c.wait_send()
        tabs.wait_send()
        for m in range(MB):
            wait_x(m).wait_send()
            for c in range(NC):
                wait_d(m, c).wait_send()
                wait_r(m, c).wait_send()
            send_out(m).wait()

    ret_t = pltpu.VMEM((SLOTS, CS, 128), BF)
    dma = pltpu.SemaphoreType.DMA
    scratch = [
        pltpu.VMEM((MB, T, D), BF),
        pltpu.VMEM((MB, T, D), BF),
        pltpu.VMEM((MB * T, SUB, 128), BF),
        pltpu.VMEM((MB * T, SUB, 128), BF),
        pltpu.VMEM((MB, SLOTS, SUB, 128), BF),
        pltpu.VMEM((MB, SLOTS, SUB, 128), BF),
        pltpu.VMEM((MB, NC, SLOTS, CS, 128), BF),
        pltpu.VMEM((MB, NC, SLOTS, CS, 128), BF),
        pltpu.VMEM((MB, NC, SLOTS, CS, 128), BF),
        pltpu.VMEM((MB, SLOTS, D), BF),
        pltpu.VMEM((SLOTS, D), BF),
        pltpu.VMEM((SLOTS, D), BF),
        pltpu.VMEM((SLOTS, CD), BF),
        pltpu.VMEM((MB, SLOTS, FF), F32),
        pltpu.VMEM((MB, SLOTS, FF), F32),
        pltpu.VMEM((MB, SLOTS, FF), F32),
        pltpu.VMEM((MB, SLOTS, 128), F32),
        pltpu.VMEM((PEERS, 16, 128), F32),
        pltpu.VMEM((PEERS, 16, 128), F32),
        pltpu.VMEM((SLOTS, 128), F32),
        pltpu.VMEM((D, FF), BF),
        pltpu.VMEM((D, FF), BF),
        pltpu.VMEM((FF, D), BF),
        pltpu.VMEM((T, SUB, 128), BF),
        pltpu.VMEM((MB, T, D), BF),
        *([ret_t] * (MB * NC)),
        dma((3,)),
        dma((3,)),
        dma((3,)),
        dma((3,)),
        dma,
        dma,
        dma((MB,)),
        dma((MB,)),
        dma((MB, NC)),
        dma((MB, NC)),
        dma((MB, NC)),
        dma((MB, NC)),
        dma((MB,)),
        dma((MB,)),
    ]
    return kernel, scratch


def on_device(section_inputs, out_grad, norm_gain, route_ids, route_weight, w_gate, w_up, w_down):
    lanes = lax.axis_size("pipe")
    peers = lax.axis_size("expert")
    micro, tok_rows, width = section_inputs.shape[1:]
    hidden = w_gate.shape[3]
    slots = peers * CAP
    ids = route_ids[0, :, :, 0]
    weights = route_weight[0, :, :, 0]
    onehot = (ids[:, :, None] == jnp.arange(peers, dtype=jnp.int32)).astype(jnp.int32)
    rank = jnp.cumsum(onehot, axis=1) - onehot
    slot = ids * CAP + jnp.sum(rank * onehot, axis=-1)
    slot_up = lax.ppermute(slot, "pipe", [((i + 2) % lanes, i) for i in range(lanes)])
    picked = slot[:, :, None] == jnp.arange(slots, dtype=jnp.int32)
    tok = jnp.sum(jnp.where(picked, jnp.arange(tok_rows, dtype=jnp.int32)[None, :, None], 0), axis=1)
    cidx = jnp.sum(jnp.where(picked, slot_up[:, :, None], 0), axis=1)
    wslot = jnp.sum(jnp.where(picked, weights[:, :, None], 0.0), axis=1)
    wtab = wslot.reshape(micro, peers, CAP).transpose(1, 0, 2).reshape(peers, micro * CAP)
    wtab = jnp.pad(wtab, ((0, 0), (0, 16 - micro * CAP)))
    wtab = jnp.broadcast_to(wtab[:, :, None], (peers, 16, 128))

    kernel, scratch = make_kernel(micro, tok_rows, width, hidden, lanes, peers)
    smem = pl.BlockSpec(memory_space=pltpu.SMEM)
    hbm = pl.BlockSpec(memory_space=pl.ANY)
    vmem = pl.BlockSpec(memory_space=pltpu.VMEM)
    out = pl.pallas_call(
        kernel,
        out_shape=jax.ShapeDtypeStruct((micro, tok_rows, width), BF),
        in_specs=[smem, smem, smem, hbm, hbm, hbm, vmem, hbm, hbm, hbm],
        out_specs=hbm,
        scratch_shapes=scratch,
        compiler_params=pltpu.CompilerParams(
            collective_id=0, has_side_effects=True, vmem_limit_bytes=58 * 1024 * 1024
        ),
        name="chain",
    )(
        tok.reshape(-1),
        cidx.reshape(-1),
        slot_up.reshape(-1),
        section_inputs[0],
        out_grad[0],
        wtab,
        norm_gain,
        w_gate[0, 0],
        w_up[0, 0],
        w_down[0, 0],
    )
    return out[None]


def solution(mesh):
    in_specs = (
        P("pipe", None, "expert", None),
        P("pipe", None, "expert", None),
        P(),
        P("pipe", None, "expert", None),
        P("pipe", None, "expert", None),
        P("pipe", "expert", None, None),
        P("pipe", "expert", None, None),
        P("pipe", "expert", None, None),
    )
    return jax.shard_map(
        on_device, mesh=mesh, in_specs=in_specs, out_specs=P("pipe", None, "expert", None), check_vma=False
    )
```

time: 1180 us -> 265 us (0.22)
  waiting for transfers between devices: 450 us -> 0.22 us
  Pallas kernels: 0 us -> 250 us
  local copies, waits for them, and re-layouts: 204 us -> 5.3 us
  blocking collectives: 150 us -> 0 us
  starting transfers between devices: 141 us -> 5.86 us
  other arithmetic: 118 us -> 3.33 us
  matrix products: 105 us -> 0 us
    ppermute x33 -> x1, waiting for transfers between devices: 269 us -> 0.22 us  [on_device(): lax.ppermute(slot, 'pipe', [((i + 2) % lanes, i) for i in range(lanes)])]
    pallas_call x0 -> x1, Pallas kernels: none -> 250 us  [on_device(): pl.pallas_call(kernel, out_shape=jax.ShapeDtypeStruct((micro, tok_rows, w...]
    all_to_all x22 -> x0, waiting for transfers between devices: 181 us -> none  [the longest x11 102 us: step(): lax.all_to_all(summed, 'expert', split_axis=0, concat_axis=0, tiled=True)]
    all_to_all x11 -> x0, blocking collectives: 150 us -> none  [step(): lax.all_to_all(x_now, 'expert', split_axis=0, concat_axis=0, tiled=True)]
    all_to_all x22 -> x0, starting transfers between devices: 124 us -> none  [the longest x11 63.1 us: step(): lax.all_to_all(d_send, 'expert', split_axis=0, concat_axis=0, tiled=True)]
    dot_general x41 -> x0, matrix products: 105 us -> none  [the longest x11 23.3 us: step(): jnp.dot(send_now, output_gradient, preferred_element_type=jnp.float32)]
    reshape x34 -> x5, local copies, waits for them, and re-layouts: 74.9 us -> 2.07 us  [the longest x1 0.68 us: on_device(): cidx.reshape(-1)]
    another operation x23 -> x0, other arithmetic: 63.1 us -> none  [the longest x11 43.1 us: step(): rows_x = jnp.stack([recv_x, other[0]])]
  transfers between devices with their start and end apart: 55 -> 1, of which waited for: 55 -> 1; matrix products, arithmetic and copies ran while one was open for 5% -> 0% of each run, Pallas kernels for 0% -> 0%
where the time goes in v1:
time: 265 us
  Pallas kernels  250 us (94%)
  starting transfers between devices  5.86 us (2%)
  local copies, waits for them, and re-layouts  5.3 us (2%)
  other arithmetic  3.33 us (1%)
    pallas_call x1, Pallas kernels, on_device(): pl.pallas_call(kernel, out_shape=jax.ShapeDtypeStruct((micro, tok_rows, w...  250 us
    ppermute x1, starting transfers between devices, on_device(): lax.ppermute(slot, 'pipe', [((i + 2) % lanes, i) for i in range(lanes)])  5.86 us
  transfers between devices with their start and end apart: 1, of which 1 were waited for; matrix products, arithmetic and copies ran while one was open for 0% of the time, Pallas kernels for 0%

profile of v1, /device:TPU:8, one launch (start us, length us, event | category | flops | bytes accessed | tf_op | source)
XLA Modules:
  0.0 264.8 jit_solution(15564521976170615967)
XLA Ops:
  0.0 0.8 fusion
  0.8 0.1 reduce_window_sum.11
  0.8 0.9 select_reduce_fusion.3
  1.7 0.7 multiply_add_fusion
  2.4 5.9 %collective-permute-start = (s32[4,32]{1,0:T(4,128)S(1)}, s32[4,32]{1,0:T(4,128)S(1)}, u32[]{:S(2)}, u32[]{:S(2)}) collective-permute-start(s32[4,32]{1,0:T(4,128)S(1)} %multiply_add_fusion), channel_id=1, source_target_pairs={{32,0},{48,16},{64,32},{80,48},{96,64},{112,80},{128,96},{144,112}... | collective-permute-start | bytes 1544 | tf_op jit(solution)/shard_map/ppermute | solution.py:351
  8.3 0.8 select_reduce_fusion
  9.1 0.1 reshape.30
  9.2 0.1 copy.11
  9.3 0.1 copy.13
  9.4 0.2 collective-permute-done
  9.6 0.1 select_reduce_fusion.1
  9.7 0.7 reshape.28.cidx_ref
  10.4 0.7 reshape.27.tok_ref
  11.1 0.6 reshape.29.slotup_ref
  11.7 0.8 broadcast_in_dim.56.wtab_hbm
  12.4 250.1 %chain.1 = bf16[4,32,4096]{2,1,0:T(8,128)(2,1)} custom-call(s32[192]{0:T(256)} %reshape.27.tok_ref, s32[192]{0:T(256)} %reshape.28.cidx_ref, s32[128]{0:T(128)} %reshape.29.slotup_ref, bf16[4,32,4096]{2,1,0:T(8,128)(2,1)} %bitcast.15, bf16[4,32,4096]{2,1,0:T(8,128)(2,1)} %bitcast.16, f32[16,16,128]{2,1,0:T(8,128)} %broadcast_in_dim.56.wtab_hbm, ...), custom_call_target="tpu_custom_call" | custom-call | tf_op jit(solution)/shard_map/chain/pallas_call | solution.py:364
  262.6 2.3 copy.15
  (2 shorter events, 0.0 us)
Async XLA Ops:
  2.4 7.2 %collective-permute-start = (s32[4,32]{1,0:T(4,128)S(1)}, s32[4,32]{1,0:T(4,128)S(1)}, u32[]{:S(2)}, u32[]{:S(2)}) collective-permute-start(s32[4,32]{1,0:T(4,128)S(1)} %multiply_add_fusion), channel_id=1, source_target_pairs={{32,0},{48,16},{64,32},{80,48},{96,64},{112,80},{128,96},{144,112}... | collective-permute-start | bytes 1544 | tf_op jit(solution)/shard_map/ppermute | solution.py:351

commit v2 on v1

v2 whole, which is shorter than its diff:
```python
import jax
import jax.numpy as jnp
from jax import lax
from jax.experimental import pallas as pl
from jax.experimental.pallas import tpu as pltpu
from jax.sharding import PartitionSpec as P

EPS = 1e-06
MESH = pl.DeviceIdType.MESH
BF = jnp.bfloat16
F32 = jnp.float32
CAP = 3
NC = 2


def dot_t(a, b):
    return lax.dot_general(a, b, (((1,), (1,)), ((), ())), preferred_element_type=F32)


def make_kernel(MB, T, D, FH, LANES, PEERS):
    SEC = LANES // 2
    SLOTS = PEERS * CAP
    SUB = D // 128
    CS = SUB // NC
    CD = D // NC
    FF = 2 * FH

    def kernel(tok_ref, cidx0_ref, cidx1_ref, slot_ref, slotup_ref, x_hbm, og_hbm, wtab_hbm, gain_ref, wg_hbm, wu_hbm, wd_hbm,
               out_hbm,
               xv, ov, xrow, orow, sendx, recvx, sendd0, sendd1, sendt1, recvd, sendr, xstd, xn, dys, ostd, fa, fb, fc, rs,
               wtab, wrecv, wrow, wg, wu, wd, wgt, wut, fin, outup, outown,
               ra0, ra1, ra2, ra3, rb0, rb1, rb2, rb3, rc0, rc1, rc2, rc3,
               in_sem, wl_sem, wrs_sem, wrr_sem, ts_sem, tr_sem, xs_sem, xr_sem, d0s_sem, d1s_sem, dts_sem, d0r_sem, d1r_sem,
               s0_sem, s1_sem, ra_sem, rb_sem, rc_sem, os_sem, or_sem, ol_sem):
        ra = (ra0, ra1, ra2, ra3)
        rb = (rb0, rb1, rb2, rb3)
        rc = (rc0, rc1, rc2, rc3)
        p = lax.axis_index("pipe")
        e = lax.axis_index("expert")
        s = p // 2
        h = p % 2
        down = (p + LANES - 2) % LANES
        up = (p + 2) % LANES
        mate = p + 1 - 2 * h
        top = s == SEC - 1
        low = jnp.logical_not(top)
        bottom = s == 0
        above = jnp.logical_not(bottom)
        both = jnp.logical_and

        def local_in(src, dst, i):
            return pltpu.make_async_copy(src, dst, in_sem.at[i])

        in_x = local_in(x_hbm, xv, 0)
        in_o = local_in(og_hbm, ov, 1)
        in_t = local_in(wtab_hbm, wtab, 2)
        in_x.start()
        in_t.start()
        in_o.start()
        part = pl.ds(pl.multiple_of(h * FH, 128), FH)
        lw = (
            pltpu.make_async_copy(wg_hbm, wg.at[:, part], wl_sem.at[0]),
            pltpu.make_async_copy(wu_hbm, wu.at[:, part], wl_sem.at[1]),
            pltpu.make_async_copy(wd_hbm, wd.at[part, :], wl_sem.at[2]),
        )
        for c in lw:
            c.start()

        barrier = pltpu.get_barrier_semaphore()

        def sig_plane(k, _):
            pl.semaphore_signal(barrier, inc=1, device_id=(p, (e + k) % PEERS), device_id_type=MESH)
            return 0

        lax.fori_loop(1, PEERS, sig_plane, 0)

        def sig_z(k, _):
            peer = (e + k) % PEERS
            pl.semaphore_signal(barrier, inc=1, device_id=(down, peer), device_id_type=MESH)
            pl.semaphore_signal(barrier, inc=1, device_id=(up, peer), device_id_type=MESH)
            return 0

        lax.fori_loop(0, PEERS, sig_z, 0)
        pl.semaphore_signal(barrier, inc=1, device_id=(mate, e), device_id_type=MESH)
        pl.semaphore_wait(barrier, PEERS - 1 + 2 * PEERS + 1)

        def rcopy(src, dst, ssem, rsem, dev):
            return pltpu.make_async_remote_copy(
                src_ref=src, dst_ref=dst, send_sem=ssem, recv_sem=rsem, device_id=dev, device_id_type=MESH
            )

        rw = (
            rcopy(wg_hbm, wg.at[:, part], wrs_sem.at[0], wrr_sem.at[0], (mate, e)),
            rcopy(wu_hbm, wu.at[:, part], wrs_sem.at[1], wrr_sem.at[1], (mate, e)),
            rcopy(wd_hbm, wd.at[part, :], wrs_sem.at[2], wrr_sem.at[2], (mate, e)),
        )
        for c in rw:
            c.start()

        mine = pl.ds(e * CAP, CAP)
        MOST = pl.ds(0, SLOTS - CAP)

        def scatter(src, dst, ssem, rsem, pipe, first):
            def go(k, _):
                peer = (e + k) % PEERS
                rcopy(src.at[pl.ds(peer * CAP, CAP)], dst.at[mine], ssem, rsem, (pipe, peer)).start()
                return 0

            lax.fori_loop(first, PEERS, go, 0)

        def arrived(buf, sem, self_too):
            v = buf if self_too else buf.at[MOST]
            return rcopy(v, v, sem, sem, (p, e)).wait_recv()

        def sent(buf, sem, self_too):
            v = buf if self_too else buf.at[MOST]
            return rcopy(v, v, sem, sem, (p, e)).wait_send()

        in_x.wait()
        in_t.wait()

        def tables(k, _):
            peer = (e + k) % PEERS
            rcopy(wtab.at[peer], wrecv.at[e], ts_sem, tr_sem, (p, peer)).start()
            return 0

        lax.fori_loop(1, PEERS, tables, 0)
        wrecv[e] = wtab[e]
        tabs = rcopy(wtab.at[pl.ds(0, PEERS - 1)], wrecv.at[pl.ds(0, PEERS - 1)], ts_sem, tr_sem, (p, e))
        in_o.wait()

        for m in range(MB):
            xrow[pl.ds(m * T, T)] = xv[m].reshape(T, SUB, 128)
            for k in range(SLOTS):
                sendx[m, k] = xrow[m * T + tok_ref[m * SLOTS + k]]
            recvx[m, mine] = sendx[m, mine]
            scatter(sendx.at[m], recvx.at[m], xs_sem.at[m], xr_sem.at[m], p, 1)

            @pl.when(top)
            def _():
                orow[pl.ds(m * T, T)] = ov[m].reshape(T, SUB, 128)
                for k in range(SLOTS):
                    sendd0[m, k] = orow[m * T + tok_ref[m * SLOTS + k], pl.ds(0, CS), :]
                recvd[m, 0, mine] = sendd0[m, mine]
                scatter(sendd0.at[m], recvd.at[m, 0], d0s_sem.at[m], d0r_sem.at[m], p, 1)
                for k in range(SLOTS):
                    sendt1[m, k] = orow[m * T + tok_ref[m * SLOTS + k], pl.ds(CS, CS), :]
                recvd[m, 1, mine] = sendt1[m, mine]
                scatter(sendt1.at[m], recvd.at[m, 1], dts_sem.at[m], d1r_sem.at[m], p, 1)

        gain = gain_ref.at[pl.ds(s, 1), :]
        QD = 512
        QE = 1024

        for c in lw:
            c.wait()
        for c in rw:
            c.wait_recv()
        tabs.wait_recv()

        def factors(m, _):
            arrived(recvx.at[m], xr_sem.at[m], False)
            xstd[m] = recvx[m].reshape(SLOTS, D)
            for j in range(CAP):
                wrow[pl.ds(j, PEERS, stride=CAP), :] = wrecv[:, m * CAP + j, :]
            w = wrow[:, :1]

            def sq(i, acc):
                col = pl.ds(pl.multiple_of(i * QD, QD), QD)
                v = xstd[m, :, col].astype(F32)
                return acc + jnp.sum(v * v, axis=-1, keepdims=True)

            total = lax.fori_loop(0, D // QD, sq, jnp.zeros((SLOTS, 1), F32))
            r = lax.rsqrt(total * (1.0 / D) + EPS)
            rs[m] = jnp.broadcast_to(r, (SLOTS, 128))

            def norm(i, _):
                col = pl.ds(pl.multiple_of(i * QD, QD), QD)
                xn[:, col] = (xstd[m, :, col].astype(F32) * r * gain[:, col]).astype(BF)
                return 0

            lax.fori_loop(0, D // QD, norm, 0)
            gate = jnp.dot(xn[...], wg[...], preferred_element_type=F32)
            upv = jnp.dot(xn[...], wu[...], preferred_element_type=F32)
            q = jax.nn.sigmoid(gate)
            a = upv * q * (1.0 + gate * (1.0 - q))
            b = gate * q
            fa[m] = w * a
            fb[m] = w * b
            fc[m] = w * (a * gate + b * upv) * (1.0 / D)
            return 0

        lax.fori_loop(0, jnp.where(top, 1, MB), factors, 0)

        @pl.when(low)
        def _():
            def flip(i, _):
                blk = pl.ds(pl.multiple_of(i * QD, QD), QD)
                wgt[:, blk] = wg[blk, :].T
                wut[:, blk] = wu[blk, :].T
                return 0

            lax.fori_loop(0, D // QD, flip, 0)

            def flipd(i, _):
                blk = pl.ds(pl.multiple_of(i * QD, QD), QD)
                wg[blk, :] = wd[:, blk].T
                return 0

            lax.fori_loop(0, D // QD, flipd, 0)

        def home0(m):
            arrived(ra[m], ra_sem.at[m], True)
            for k in range(SLOTS):
                sendd0[m, k] = ra[m][cidx0_ref[m * SLOTS + k]]
            recvd[m, 0, mine] = sendd0[m, mine]
            scatter(sendd0.at[m], recvd.at[m, 0], d0s_sem.at[m], d0r_sem.at[m], p, 1)

        def home1(m):
            for k in range(SLOTS):
                sendd1[m, k] = rb[m][cidx1_ref[m * SLOTS + k]]
            scatter(sendd1.at[m], recvd.at[m, 1], d1s_sem.at[m], d1r_sem.at[m], down, 0)

        def send_up(m):
            return rcopy(outup.at[m], out_hbm.at[m, :, pl.ds(0, CD)], os_sem.at[m], or_sem.at[m], (up, e))

        def own_out(m, c):
            return pltpu.make_async_copy(outown.at[m, c], out_hbm.at[m, :, pl.ds(c * CD, CD)], ol_sem.at[m, c])

        def expert(m, flat):
            arrived(recvd.at[m, 0], d0r_sem.at[m], False)

            def partial(c):
                dys[:, c * CD:(c + 1) * CD] = recvd[m, c].reshape(SLOTS, CD)
                v = dys[:, c * CD:(c + 1) * CD]
                if flat:
                    return jnp.dot(v, wg[c * CD:(c + 1) * CD, :], preferred_element_type=F32)
                return dot_t(v, wd[:, c * CD:(c + 1) * CD])

            da = partial(0)
            arrived(recvd.at[m, 1], d1r_sem.at[m], flat)
            da = da + partial(1)
            dg = (da * fa[m]).astype(BF)
            du = (da * fb[m]).astype(BF)
            r = rs[m][:, :1]
            mean = jnp.sum(da * fc[m], axis=-1, keepdims=True) * (r * r)
            for c in (1, 0):
                for i in range(CD // QE):
                    col = pl.ds(c * CD + i * QE, QE)
                    if flat:
                        con = jnp.dot(dg, wgt[:, col], preferred_element_type=F32)
                        con = con + jnp.dot(du, wut[:, col], preferred_element_type=F32)
                    else:
                        con = dot_t(dg, wg[col, :]) + dot_t(du, wu[col, :])
                    res = dys[:, col].astype(F32) + (con * gain[:, col]) * r - xstd[m, :, col].astype(F32) * mean
                    ostd[:, pl.ds(i * QE, QE)] = res.astype(BF)
                sendr[m, c] = ostd[...].reshape(SLOTS, CS, 128)
                for i in range(MB):

                    @pl.when(m == i)
                    def _():
                        if c == 1:
                            rb[i][mine] = sendr[i, 1, mine]
                            scatter(sendr.at[i, 1], rb[i], s1_sem.at[i], rb_sem.at[i], p, 1)
                        else:
                            if flat:

                                @pl.when(above)
                                def _():
                                    scatter(sendr.at[i, 0], ra[i], s0_sem.at[i], ra_sem.at[i], down, 0)

                                @pl.when(bottom)
                                def _():
                                    rc[i][mine] = sendr[i, 0, mine]
                                    scatter(sendr.at[i, 0], rc[i], s0_sem.at[i], rc_sem.at[i], p, 1)

                            else:
                                scatter(sendr.at[i, 0], ra[i], s0_sem.at[i], ra_sem.at[i], down, 0)

        def output(m):
            @pl.when(low)
            def _():
                for t in range(T):
                    fin[t] = ra[m][slotup_ref[m * T + t]]
                outup[m] = fin[...].reshape(T, CD)
                send_up(m).start()

            for t in range(T):
                fin[t] = rb[m][slot_ref[m * T + t]]
            outown[m, 1] = fin[...].reshape(T, CD)
            own_out(m, 1).start()

        @pl.when(low)
        def _():
            home0(0)

        def chain(m, _):
            @pl.when(top)
            def _():
                expert(m, False)

            @pl.when(low)
            def _():
                expert(m, True)

            lax.fori_loop(m + 1, jnp.where(both(top, m < MB - 1), m + 2, m + 1), factors, 0)
            for i in range(MB):

                @pl.when(m == i)
                def _():
                    if i + 1 < MB:

                        @pl.when(low)
                        def _():
                            home0(i + 1)

                    arrived(rb[i], rb_sem.at[i], False)

                    @pl.when(above)
                    def _():
                        home1(i)

                    output(i)

            return 0

        lax.fori_loop(0, MB, chain, 0)

        @pl.when(bottom)
        def _():
            for m in range(MB):
                arrived(rc[m], rc_sem.at[m], False)
                for t in range(T):
                    fin[t] = rc[m][slot_ref[m * T + t]]
                outown[m, 0] = fin[...].reshape(T, CD)
                own_out(m, 0).start()

        for c in rw:
            c.wait_send()
        tabs.wait_send()
        for m in range(MB):
            sent(sendx.at[m], xs_sem.at[m], False)
            sent(sendd0.at[m], d0s_sem.at[m], False)
            sent(sendr.at[m, 1], s1_sem.at[m], False)
            own_out(m, 1).wait()

            @pl.when(top)
            def _():
                sent(sendt1.at[m], dts_sem.at[m], False)

            @pl.when(low)
            def _():
                send_up(m).wait_send()

            @pl.when(above)
            def _():
                sent(sendd1.at[m], d1s_sem.at[m], True)
                sent(sendr.at[m, 0], s0_sem.at[m], True)
                send_up(m).wait_recv()

            @pl.when(bottom)
            def _():
                sent(sendr.at[m, 0], s0_sem.at[m], False)
                own_out(m, 0).wait()

    half_t = pltpu.VMEM((SLOTS, CS, 128), BF)
    halves = pltpu.VMEM((MB, SLOTS, CS, 128), BF)
    dma = pltpu.SemaphoreType.DMA
    scratch = [
        pltpu.VMEM((MB, T, D), BF),
        pltpu.VMEM((MB, T, D), BF),
        pltpu.VMEM((MB * T, SUB, 128), BF),
        pltpu.VMEM((MB * T, SUB, 128), BF),
        pltpu.VMEM((MB, SLOTS, SUB, 128), BF),
        pltpu.VMEM((MB, SLOTS, SUB, 128), BF),
        halves,
        halves,
        halves,
        pltpu.VMEM((MB, NC, SLOTS, CS, 128), BF),
        pltpu.VMEM((MB, NC, SLOTS, CS, 128), BF),
        pltpu.VMEM((MB, SLOTS, D), BF),
        pltpu.VMEM((SLOTS, D), BF),
        pltpu.VMEM((SLOTS, D), BF),
        pltpu.VMEM((SLOTS, CD), BF),
        pltpu.VMEM((MB, SLOTS, FF), F32),
        pltpu.VMEM((MB, SLOTS, FF), F32),
        pltpu.VMEM((MB, SLOTS, FF), F32),
        pltpu.VMEM((MB, SLOTS, 128), F32),
        pltpu.VMEM((PEERS, 16, 128), F32),
        pltpu.VMEM((PEERS, 16, 128), F32),
        pltpu.VMEM((SLOTS, 128), F32),
        pltpu.VMEM((D, FF), BF),
        pltpu.VMEM((D, FF), BF),
        pltpu.VMEM((FF, D), BF),
        pltpu.VMEM((FF, D), BF),
        pltpu.VMEM((FF, D), BF),
        pltpu.VMEM((T, CS, 128), BF),
        pltpu.VMEM((MB, T, CD), BF),
        pltpu.VMEM((MB, NC, T, CD), BF),
        *([half_t] * (3 * MB)),
        dma((3,)),
        dma((3,)),
        dma((3,)),
        dma((3,)),
        dma,
        dma,
        *([dma((MB,))] * 14),
        dma((MB, NC)),
    ]
    return kernel, scratch


def on_device(section_inputs, out_grad, norm_gain, route_ids, route_weight, w_gate, w_up, w_down):
    lanes = lax.axis_size("pipe")
    peers = lax.axis_size("expert")
    micro, tok_rows, width = section_inputs.shape[1:]
    hidden = w_gate.shape[3]
    slots = peers * CAP
    ids = route_ids[0, :, :, 0]
    weights = route_weight[0, :, :, 0]
    onehot = (ids[:, :, None] == jnp.arange(peers, dtype=jnp.int32)).astype(jnp.int32)
    rank = jnp.cumsum(onehot, axis=1) - onehot
    slot = ids * CAP + jnp.sum(rank * onehot, axis=-1)
    slot_up = lax.ppermute(slot, "pipe", [((i + 2) % lanes, i) for i in range(lanes)])
    picked = slot[:, :, None] == jnp.arange(slots, dtype=jnp.int32)
    tok = jnp.sum(jnp.where(picked, jnp.arange(tok_rows, dtype=jnp.int32)[None, :, None], 0), axis=1)
    cidx = jnp.sum(jnp.where(picked, slot_up[:, :, None], 0), axis=1)
    cidx_down = lax.ppermute(cidx, "pipe", [(i, (i + 2) % lanes) for i in range(lanes)])
    wslot = jnp.sum(jnp.where(picked, weights[:, :, None], 0.0), axis=1)
    wtab = wslot.reshape(micro, peers, CAP).transpose(1, 0, 2).reshape(peers, micro * CAP)
    wtab = jnp.pad(wtab, ((0, 0), (0, 16 - micro * CAP)))
    wtab = jnp.broadcast_to(wtab[:, :, None], (peers, 16, 128))

    kernel, scratch = make_kernel(micro, tok_rows, width, hidden, lanes, peers)
    smem = pl.BlockSpec(memory_space=pltpu.SMEM)
    hbm = pl.BlockSpec(memory_space=pl.ANY)
    vmem = pl.BlockSpec(memory_space=pltpu.VMEM)
    out = pl.pallas_call(
        kernel,
        out_shape=jax.ShapeDtypeStruct((micro, tok_rows, width), BF),
        in_specs=[smem, smem, smem, smem, smem, hbm, hbm, hbm, vmem, hbm, hbm, hbm],
        out_specs=hbm,
        scratch_shapes=scratch,
        compiler_params=pltpu.CompilerParams(
            collective_id=0, has_side_effects=True, vmem_limit_bytes=58 * 1024 * 1024
        ),
        name="chain",
    )(
        tok.reshape(-1),
        cidx.reshape(-1),
        cidx_down.reshape(-1),
        slot.reshape(-1),
        slot_up.reshape(-1),
        section_inputs[0],
        out_grad[0],
        wtab,
        norm_gain,
        w_gate[0, 0],
        w_up[0, 0],
        w_down[0, 0],
    )
    return out[None]


def solution(mesh):
    in_specs = (
        P("pipe", None, "expert", None),
        P("pipe", None, "expert", None),
        P(),
        P("pipe", None, "expert", None),
        P("pipe", None, "expert", None),
        P("pipe", "expert", None, None),
        P("pipe", "expert", None, None),
        P("pipe", "expert", None, None),
    )
    return jax.shard_map(
        on_device, mesh=mesh, in_specs=in_specs, out_specs=P("pipe", None, "expert", None), check_vma=False
    )
```

time: 265 us -> 241 us (0.909)
  Pallas kernels: 250 us -> 221 us
    pallas_call x1, Pallas kernels: 250 us -> 221 us  [on_device(): pl.pallas_call(kernel, out_shape=jax.ShapeDtypeStruct((micro, tok_rows, w...]
  transfers between devices with their start and end apart: 1 -> 2, of which waited for: 1 -> 2; matrix products, arithmetic and copies ran while one was open for 0% -> 2% of each run, Pallas kernels for 0% -> 0%
where the time goes in v2:
time: 241 us; the launch traced here: 239 us
  Pallas kernels  221 us (92%)
  local copies, waits for them, and re-layouts  6.04 us (3%)
  starting transfers between devices  5.94 us (2%)
  other arithmetic  4.62 us (2%)
    pallas_call x1, Pallas kernels, on_device(): pl.pallas_call(kernel, out_shape=jax.ShapeDtypeStruct((micro, tok_rows, w...  221 us
    ppermute x1, starting transfers between devices, on_device(): lax.ppermute(slot, 'pipe', [((i + 2) % lanes, i) for i in range(lanes)])  5.86 us
  transfers between devices with their start and end apart: 2, of which 2 were waited for; matrix products, arithmetic and copies ran while one was open for 2% of the time, Pallas kernels for 0%

profile of v2, /device:TPU:8, one launch (start us, length us, event | category | flops | bytes accessed | tf_op | source)
XLA Modules:
  0.0 239.4 jit_solution(18151834771419882660)
XLA Ops:
  0.0 0.8 fusion
  0.8 0.1 reduce_window_sum.11
  0.8 0.9 select_reduce_fusion.3
  1.7 0.7 multiply_add_fusion
  2.4 5.9 %collective-permute-start = (s32[4,32]{1,0:T(4,128)S(1)}, s32[4,32]{1,0:T(4,128)S(1)}, u32[]{:S(2)}, u32[]{:S(2)}) collective-permute-start(s32[4,32]{1,0:T(4,128)S(1)} %multiply_add_fusion), channel_id=1, source_target_pairs={{32,0},{48,16},{64,32},{80,48},{96,64},{112,80},{128,96},{144,112}... | collective-permute-start | bytes 1544 | tf_op jit(solution)/shard_map/ppermute | solution.py:424
  8.3 0.8 select_reduce_fusion
  9.1 0.5 collective-permute-done
  9.6 0.1 select_reduce_fusion.1
  9.7 0.1 collective-permute-start.1
  9.8 0.7 multiply_reduce_fusion
  10.5 0.1 reduce_sum.41
  10.6 0.1 mul.26
  10.7 0.1 reshape.39
  10.8 0.1 copy.11
  10.9 0.1 copy.13
  11.0 0.6 add.13.slot_ref
  11.6 0.7 reshape.36.cidx0_ref
  12.2 0.7 reshape.35.tok_ref
  12.9 0.6 reshape.38.slotup_ref
  13.5 1.4 collective-permute-done.1
  14.8 0.6 reshape.37.cidx1_ref
  15.5 0.8 broadcast_in_dim.56.wtab_hbm
  16.2 220.9 %chain.1 = bf16[4,32,4096]{2,1,0:T(8,128)(2,1)} custom-call(s32[192]{0:T(256)} %reshape.35.tok_ref, s32[192]{0:T(256)} %reshape.36.cidx0_ref, s32[192]{0:T(256)} %reshape.37.cidx1_ref, s32[128]{0:T(128)} %add.13.slot_ref, s32[128]{0:T(128)} %reshape.38.slotup_ref, bf16[4,32,4096]{2,1,0:T(8,128)(2,1)} %bitcast.15, bf16[4,32,4096]{2,1,0:T(8,128)(2,1)} %bitcast.16, ...), custom_call_target="tpu_custom_call" | custom-call | tf_op jit(solution)/shard_map/chain/pallas_call | solution.py:438
  237.1 2.3 copy.15
  (2 shorter events, 0.0 us)
Async XLA Ops:
  2.4 7.2 %collective-permute-start = (s32[4,32]{1,0:T(4,128)S(1)}, s32[4,32]{1,0:T(4,128)S(1)}, u32[]{:S(2)}, u32[]{:S(2)}) collective-permute-start(s32[4,32]{1,0:T(4,128)S(1)} %multiply_add_fusion), channel_id=1, source_target_pairs={{32,0},{48,16},{64,32},{80,48},{96,64},{112,80},{128,96},{144,112}... | collective-permute-start | bytes 1544 | tf_op jit(solution)/shard_map/ppermute | solution.py:424
  9.7 5.1 %collective-permute-start.1 = (s32[4,48]{1,0:T(4,128)S(1)}, s32[4,48]{1,0:T(4,128)S(1)}, u32[]{:S(2)}, u32[]{:S(2)}) collective-permute-start(s32[4,48]{1,0:T(4,128)S(1)} %get-tuple-element.5), channel_id=1, source_target_pairs={{0,32},{16,48},{32,64},{48,80},{64,96},{80,112},{96,128},{112,144}... | collective-permute-start | bytes 2312 | tf_op jit(solution)/shard_map/ppermute | solution.py:428
